TPU v7x, 32 devices: a whole 2x2x4 slice. The times are simulated.
32 devices in a mesh: grp: 2 (over y), row: 4 (over x, core), col: 4 (over z).
Axes of the slice: x: 2, y: 2, z: 4, core: 2. Of those that a mesh axis runs over, the one named last changes fastest.
Arguments:
- programs: bfloat16 [2048, 2048], P(('grp', 'row'), 'col'), parts along dimension 0, may hold values from -6 to 6
- tests: bfloat16 [2048, 2048], P(('grp', 'col'), 'row'), parts along dimension 0, may hold values from -6 to 6
- weight: bfloat16 [2048, 2048], P('col', 'row'), may hold values from -0.125 to 0.125
- labels: int32 [2048, 1024], P(('grp', 'row'), 'col'), parts along dimension 0, may hold values 0 or 1
Outputs:
- grad_programs: bfloat16 [2048, 2048], P(('grp', 'row'), 'col'), parts along dimension 0
- grad_tests: bfloat16 [2048, 2048], P(('grp', 'col'), 'row'), parts along dimension 0
- grad_weight: float32 [4096, 2048], P(('grp', 'col'), 'row'), parts along dimension 0
There are 2 independent parts, one for each index of `grp`. A program takes and returns all parts, laid end to end along the dimension named above; an argument that names none is the same for every part. Nothing has to cross between parts.
All inputs are finite; a program needn't handle non-finite values. No bound on the sum of `labels` on one device may be relied on, other than what follows from the above.
Results may differ from a plain program's by a relative error of at most 0.017.
Values may be sent and summed in bfloat16 or wider, within the bound.
A program may use at most 64 MiB of HBM per device.

v0:
```python
import math

import jax
import jax.numpy as jnp
from jax import lax
from jax.sharding import PartitionSpec as P

E = 2048


def contract(left, right, left_dim, right_dim):
    return lax.dot_general(
        left, right, (((left_dim,), (right_dim,)), ((), ())), preferred_element_type=jnp.float32
    )


def local(programs, tests, weight, labels):
    factor = 1.0 / math.sqrt(E)
    targets = labels.astype(jnp.float32)
    w_rows = lax.all_gather(weight, "row", axis=1, tiled=True)
    share = lax.psum_scatter(
        jnp.dot(programs, w_rows, preferred_element_type=jnp.float32).astype(jnp.bfloat16),
        "col",
        scatter_dimension=0,
        tiled=True,
    )
    projected = lax.all_gather(share, "col", axis=0, tiled=True)
    test_whole = lax.all_gather(tests, "row", axis=1, tiled=True)
    logits = contract(projected, test_whole, 1, 1) * factor
    dlogits = (jax.nn.sigmoid(logits) - targets).astype(jnp.bfloat16)
    partial_sums = jnp.dot(dlogits, test_whole, preferred_element_type=jnp.float32)
    summed = lax.psum(partial_sums.astype(jnp.bfloat16), "col")
    grad_programs = (contract(summed, w_rows, 1, 1) * factor).astype(jnp.bfloat16)
    weight_part = contract(programs, summed, 0, 0) * factor
    test_part = contract(dlogits, projected, 0, 0) * factor
    grad_weight, test_total = (
        lax.psum_scatter(
            weight_part.astype(jnp.bfloat16), "row", scatter_dimension=1, tiled=True
        ).astype(jnp.float32),
        lax.psum_scatter(
            test_part.astype(jnp.bfloat16), "row", scatter_dimension=1, tiled=True
        ).astype(jnp.float32),
    )
    grad_tests = test_total.astype(jnp.bfloat16)
    return (grad_programs, grad_tests, grad_weight)


def solution(mesh):
    placed = (
        P(("grp", "row"), "col"),
        P(("grp", "col"), "row"),
        P("col", "row"),
        P(("grp", "row"), "col"),
    )
    return jax.shard_map(
        local,
        mesh=mesh,
        in_specs=placed,
        out_specs=(P(("grp", "row"), "col"), P(("grp", "col"), "row"), P(("grp", "col"), "row")),
        check_vma=False,
    )
```

profile of v0, /device:TPU:9, one launch (start us, length us, event | category | flops | bytes accessed | tf_op | source)
XLA Modules:
  0.0 234.8 jit_solution(9814701826729110321)
XLA Ops:
  7.2 0.0 all-gather.4.cloned.1.call-start
  7.2 0.7 all-gather.4.cloned.1.call-update
  7.9 0.0 reduce-scatter.4.cloned.1.call-start
  8.0 25.8 %all-gather.4.cloned.1.call-done = bf16[512,2048]{1,0:T(8,128)(2,1)} async-done(((bf16[512,512]{1,0:T(8,128)(2,1)}), bf16[512,2048]{1,0:T(8,128)(2,1)}) %all-gather.4.cloned.1.call-update) | async-done | bytes 2097168 | tf_op jit(solution)/shard_map/all_gather | solution.py:20
  33.8 3.3 %convolution_convert_fusion = bf16[256,2048]{1,0:T(8,128)(2,1)} fusion(bf16[256,512]{1,0:T(8,128)(2,1)S(1)} %copy-done, bf16[512,2048]{1,0:T(8,128)(2,1)} %all-gather.4.cloned.1.call-done), kind=kOutput, calls=%fused_computation.3 | convolution fusion | flops 537395200 | bytes 3407872 | tf_op jit(solution)/shard_map/dot_general | solution.py:22
  37.1 0.0 all-gather.8.cloned.1.call-start
  37.1 0.7 all-gather.8.cloned.1.call-update
  37.8 0.0 all-gather.6.cloned.1.call-start
  37.8 24.1 %reduce-scatter.4.cloned.1.call-done = bf16[64,2048]{1,0:T(8,128)(2,1)} async-done(((bf16[256,2048]{1,0:T(8,128)(2,1)}), bf16[64,2048]{1,0:T(8,128)(2,1)}) %reduce-scatter.4.cloned.1.call-update) | async-done | bytes 262160 | tf_op jit(solution)/shard_map/reduce_scatter | solution.py:21
  62.0 0.0 all-reduce.2.cloned.1.call-start
  62.0 19.4 %all-gather.8.cloned.1.call-done = bf16[256,2048]{1,0:T(8,128)(2,1)} async-done(((bf16[256,512]{1,0:T(8,128)(2,1)}), bf16[256,2048]{1,0:T(8,128)(2,1)}) %all-gather.8.cloned.1.call-update) | async-done | bytes 1048592 | tf_op jit(solution)/shard_map/all_gather | solution.py:28
  81.4 28.8 %all-gather.6.cloned.1.call-done = bf16[256,2048]{1,0:T(8,128)(2,1)} async-done(((bf16[64,2048]{1,0:T(8,128)(2,1)}), bf16[256,2048]{1,0:T(8,128)(2,1)}) %all-gather.6.cloned.1.call-update) | async-done | bytes 1048592 | tf_op jit(solution)/shard_map/all_gather | solution.py:27
  110.2 2.0 fusion.8
  112.3 1.4 convolution_convert_fusion.1
  113.7 0.0 reduce-scatter.8.cloned.1.call-start
  113.8 51.3 %all-reduce.2.cloned.1.call-done = bf16[256,2048]{1,0:T(8,128)(2,1)} async-done(((bf16[256,2048]{1,0:T(8,128)(2,1)}), bf16[256,2048]{1,0:T(8,128)(2,1)}) %all-reduce.2.cloned.1.call-update) | async-done | bytes 1048592 | tf_op jit(solution)/shard_map/psum | solution.py:32
  165.1 3.3 %fusion = bf16[512,2048]{0,1:T(8,128)(2,1)} fusion(bf16[256,2048]{1,0:T(8,128)(2,1)} %all-reduce.2.cloned.1.call-done, bf16[256,512]{1,0:T(8,128)(2,1)S(1)} %copy-done), kind=kOutput, calls=%fused_computation.1 | convolution fusion | flops 538968064 | bytes 3407872 | tf_op jit(solution)/shard_map/dot_general | solution.py:12
  168.4 0.0 reduce-scatter.6.cloned.1.call-start
  168.4 1.1 copy-done.2
  169.6 1.4 fusion.1
  171.0 2.7 %fusion.2 = bf16[256,512]{1,0:T(8,128)(2,1)} fusion(bf16[256,2048]{1,0:T(8,128)(2,1)} %all-reduce.2.cloned.1.call-done, bf16[512,2048]{1,0:T(8,128)(2,1)S(1)} %copy-done.1), kind=kOutput, calls=%fused_computation.7 | convolution fusion | flops 537133056 | bytes 3407872 | tf_op jit(solution)/shard_map/dot_general | solution.py:12
  173.7 26.0 %reduce-scatter.8.cloned.1.call-done = bf16[512,512]{0,1:T(8,128)(2,1)} async-done(((bf16[512,2048]{0,1:T(8,128)(2,1)}), bf16[512,512]{0,1:T(8,128)(2,1)}) %reduce-scatter.8.cloned.1.call-update) | async-done | bytes 524304 | tf_op jit(solution)/shard_map/reduce_scatter | solution.py:37
  199.7 2.2 copy.7
  201.9 26.0 %reduce-scatter.6.cloned.1.call-done = bf16[256,512]{1,0:T(8,128)(2,1)} async-done(((bf16[256,2048]{1,0:T(8,128)(2,1)}), bf16[256,512]{1,0:T(8,128)(2,1)}) %reduce-scatter.6.cloned.1.call-update) | async-done | bytes 262160 | tf_op jit(solution)/shard_map/reduce_scatter | solution.py:40
  (14 shorter events, 0.1 us)
Async XLA Ops:
  7.2 26.6 %copy-start = (bf16[256,512]{1,0:T(8,128)(2,1)S(1)}, bf16[256,512]{1,0:T(8,128)(2,1)}, u32[]{:S(2)}) copy-start(bf16[256,512]{1,0:T(8,128)(2,1)} %param.4) | copy-start | bytes 786436
  7.2 26.6 %all-gather.4.cloned.1.call-start = ((), (), s32[]{:S(2)}) async-start(), calls=%async_computation.3 | async-start | bytes 2621440 | tf_op jit(solution)/shard_map/all_gather | solution.py:20
  7.9 102.3 %copy-start.4 = (s32[256,256]{1,0:T(8,128)S(1)}, s32[256,256]{1,0:T(8,128)}, u32[]{:S(2)}) copy-start(s32[256,256]{1,0:T(8,128)} %param.7) | copy-start | bytes 786436
  7.9 54.0 %reduce-scatter.4.cloned.1.call-start = ((), (), s32[]{:S(2)}) async-start(), calls=%async_computation.4 | async-start | bytes 1310720 | tf_op jit(solution)/shard_map/reduce_scatter | solution.py:21
  37.1 44.4 %all-gather.8.cloned.1.call-start = ((), (), s32[]{:S(2)}) async-start(), calls=%async_computation.6 | async-start | bytes 1310720 | tf_op jit(solution)/shard_map/all_gather | solution.py:28
  37.8 72.4 %all-gather.6.cloned.1.call-start = ((), (), s32[]{:S(2)}) async-start(), calls=%async_computation.5 | async-start | bytes 1310720 | tf_op jit(solution)/shard_map/all_gather | solution.py:27
  62.0 103.1 %all-reduce.2.cloned.1.call-start = ((), (), s32[]{:S(2)}) async-start(), calls=%async_computation.7 | async-start | bytes 2097152 | tf_op jit(solution)/shard_map/psum | solution.py:32
  81.4 30.9 %copy-start.3 = (bf16[256,2048]{1,0:T(8,128)(2,1)S(1)}, bf16[256,2048]{1,0:T(8,128)(2,1)}, u32[]{:S(2)}) copy-start(bf16[256,2048]{1,0:T(8,128)(2,1)} %all-gather.8.cloned.1.call-done) | copy-start | bytes 3145732
  113.7 86.0 %reduce-scatter.8.cloned.1.call-start = ((), (), s32[]{:S(2)}) async-start(), calls=%async_computation.9 | async-start | bytes 2621440 | tf_op jit(solution)/shard_map/reduce_scatter | solution.py:37
  168.4 1.2 copy-start.2
  168.4 2.7 %copy-start.1 = (bf16[512,2048]{1,0:T(8,128)(2,1)S(1)}, bf16[512,2048]{1,0:T(8,128)(2,1)}, u32[]{:S(2)}) copy-start(bf16[512,2048]{1,0:T(8,128)(2,1)} %all-gather.4.cloned.1.call-done) | copy-start | bytes 6291460
  168.4 59.5 %reduce-scatter.6.cloned.1.call-start = ((), (), s32[]{:S(2)}) async-start(), calls=%async_computation.8 | async-start | bytes 1310720 | tf_op jit(solution)/shard_map/reduce_scatter | solution.py:40
Sparse Core Ops, SparseCore 0:
  9.6 24.1 all-gather.3
  37.2 24.7 reduce-scatter.3
  63.6 17.7 all-gather.7
  82.9 27.2 all-gather.5
  113.8 51.1 all-reduce.1
  168.5 31.1 reduce-scatter.7
  203.0 24.8 reduce-scatter.5
where the time goes:
time: 237 us; the launch traced here: 235 us
  waiting for transfers between devices  203 us (86%)
  between operations  14.2 us (6%)
  matrix products  14.1 us (6%)
  local copies, waits for them, and re-layouts  3.38 us (1%)
    psum x1, waiting for transfers between devices, local(): summed = lax.psum(partial_sums.astype(jnp.bfloat16), 'col')  51.3 us
    all_gather x1, waiting for transfers between devices, local(): projected = lax.all_gather(share, 'col', axis=0, tiled=True)  28.8 us
    reduce_scatter x1, waiting for transfers between devices, local(): lax.psum_scatter(weight_part.astype(jnp.bfloat16), 'row', scatter_dimensi...  26 us
    reduce_scatter x1, waiting for transfers between devices, local(): lax.psum_scatter(test_part.astype(jnp.bfloat16), 'row', scatter_dimension...  26 us
    all_gather x1, waiting for transfers between devices, local(): w_rows = lax.all_gather(weight, 'row', axis=1, tiled=True)  25.8 us
    reduce_scatter x1, waiting for transfers between devices, local(): lax.psum_scatter(jnp.dot(programs, w_rows, preferred_element_type=jnp.flo...  24.1 us
    all_gather x1, waiting for transfers between devices, local(): test_whole = lax.all_gather(tests, 'row', axis=1, tiled=True)  19.4 us
    dot_general x4, matrix products, contract(): lax.dot_general(left, right, (((left_dim,), (right_dim,)), ((), ())), pre...  9.43 us
  transfers between devices with their start and end apart: 7, of which 7 were waited for; matrix products, arithmetic and copies ran while one was open for 3% of the time, Pallas kernels for 0%

commit v1 on v0

v1 whole, which is shorter than its diff:
```python
import functools
import math

import jax
import jax.numpy as jnp
from jax import lax
from jax.experimental import pallas as pl
from jax.experimental.pallas import tpu as pltpu
from jax.sharding import PartitionSpec as P

E = 2048
MESH = pl.DeviceIdType.MESH
BF16 = jnp.bfloat16
F32 = jnp.float32


def contract(left, right, left_dim, right_dim):
    return lax.dot_general(
        left, right, (((left_dim,), (right_dim,)), ((), ())), preferred_element_type=F32
    )


def partner(index, step):
    bit = 1
    while bit <= step:
        if step & bit:
            index = index + bit - 2 * bit * (lax.div(index, bit) % 2)
        bit *= 2
    return index


def each(count, body):
    if count <= 4:
        for k in range(1, count):
            body(k)
    else:
        lax.fori_loop(1, count, lambda k, x: (body(k), x)[1], 0)


def kernel(
    rows, cols,
    p_ref, t_ref, w_ref, l_ref,
    gp_ref, gt_ref, gw_ref,
    t_all, m_part, m_recv, m_all, l_part, l_recv, d_all, q_part, q_recv, q_all, g_part, g_recv,
    acc, send, recv,
):
    factor = 1.0 / math.sqrt(E)
    r, c = lax.axis_index("row"), lax.axis_index("col")
    t_send, ms_send, ma_send, l_send, d_send, qs_send, qa_send, g_send = (send.at[i] for i in range(8))
    t_recv, ms_recv, ma_recv, lr_recv, d_recv, qs_recv, qa_recv, gr_recv = (recv.at[i] for i in range(8))
    sub = m_part.shape[2]

    def row_peer(k):
        return {"row": lax.rem(r + k, rows)}

    def col_peer(s):
        return {"col": partner(c, s)}

    barrier = pltpu.get_barrier_semaphore()
    each(rows, lambda k: pl.semaphore_signal(barrier, inc=1, device_id=row_peer(k), device_id_type=MESH))
    for s in range(1, cols):
        pl.semaphore_signal(barrier, inc=1, device_id=col_peer(s), device_id_type=MESH)
    pl.semaphore_wait(barrier, rows - 1 + cols - 1)

    def copy_col(src, dst, s, ssem, rsem):
        return pltpu.make_async_remote_copy(
            src_ref=src, dst_ref=dst, send_sem=ssem.at[s], recv_sem=rsem.at[s],
            device_id=col_peer(s), device_id_type=MESH,
        )

    def drain(ref, sem):
        pltpu.make_async_copy(ref, ref, sem).wait()

    for s in range(1, cols):
        copy_col(t_ref, t_all.at[s - 1], s, t_send, t_recv).start()

    def scatter(part, into, s, ssem, rsem):
        def one(k):
            pltpu.make_async_remote_copy(
                src_ref=part.at[s, lax.rem(r + k, rows)], dst_ref=into.at[s, k - 1],
                send_sem=ssem.at[s], recv_sem=rsem.at[s],
                device_id=row_peer(k), device_id_type=MESH,
            ).start()
        each(rows, one)

    def gather(full, s, ssem, rsem):
        def one(k):
            pltpu.make_async_remote_copy(
                src_ref=full.at[s, r], dst_ref=full.at[s, r],
                send_sem=ssem.at[s], recv_sem=rsem.at[s],
                device_id=row_peer(k), device_id_type=MESH,
            ).start()
        each(rows, one)

    def reduce_share(part, came, full, s, ssem, rsem, rs_sem):
        drain(came.at[s], rs_sem.at[s])
        total = part[s, r].astype(F32)
        for k in range(rows - 1):
            total = total + came[s, k].astype(F32)
        full[s, r] = total.astype(BF16)
        gather(full, s, ssem, rsem)

    def whole(full, s):
        return full[s].reshape(rows * sub, full.shape[3])

    def tests_of(s):
        return t_ref[...] if s == 0 else t_all[s - 1]

    def m_make(s):
        if s:
            drain(t_all.at[s - 1], t_recv.at[s])
        part = contract(tests_of(s), w_ref[...], 1, 1)
        m_part[s] = part.astype(BF16).reshape(m_part.shape[1:])
        scatter(m_part, m_recv, s, ms_send, ms_recv)

    def m_sum(s):
        reduce_share(m_part, m_recv, m_all, s, ma_send, ma_recv, ms_recv)

    def m_use(s):
        drain(m_all.at[s, pl.ds(0, rows - 1)], ma_recv.at[s])
        part = contract(p_ref[...], whole(m_all, s), 1, 1)
        if s == 0:
            acc[...] = part
        else:
            l_part[s - 1] = part.astype(BF16)
            copy_col(l_part.at[s - 1], l_recv.at[s - 1], s, l_send, lr_recv).start()

    for s in range(cols + 2):
        if s < cols:
            m_make(s)
        if 0 <= s - 1 < cols:
            m_sum(s - 1)
        if 0 <= s - 2 < cols:
            m_use(s - 2)

    logits = acc[...]
    for s in range(1, cols):
        drain(l_recv.at[s - 1], lr_recv.at[s])
        logits = logits + l_recv[s - 1].astype(F32)
    d_all[0] = (jax.nn.sigmoid(logits * factor) - l_ref[...].astype(F32)).astype(BF16)
    for s in range(1, cols):
        copy_col(d_all.at[0], d_all.at[s], s, d_send, d_recv).start()

    def q_make(s):
        if s:
            drain(d_all.at[s], d_recv.at[s])
        part = contract(d_all[s], p_ref[...], 0, 0)
        q_part[s] = part.astype(BF16).reshape(q_part.shape[1:])
        scatter(q_part, q_recv, s, qs_send, qs_recv)

    def q_sum(s):
        reduce_share(q_part, q_recv, q_all, s, qa_send, qa_recv, qs_recv)

    def q_use(s):
        drain(q_all.at[s, pl.ds(0, rows - 1)], qa_recv.at[s])
        part = contract(whole(q_all, s), w_ref[...], 1, 0)
        if s == 0:
            g_part[0] = part.astype(BF16)
        else:
            g_part[s] = part.astype(BF16)
            copy_col(g_part.at[s], g_recv.at[s - 1], s, g_send, gr_recv).start()

    for s in range(cols + 2):
        if s < cols:
            q_make(s)
        if 0 <= s - 1 < cols:
            q_sum(s - 1)
        if 0 <= s - 2 < cols:
            q_use(s - 2)

    total = contract(d_all[0], whole(m_all, 0), 1, 0)
    for s in range(1, cols):
        total = total + contract(d_all[s], whole(m_all, s), 1, 0)
    gp_ref[...] = (total * factor).astype(BF16)
    total = contract(whole(q_all, 0), tests_of(0), 0, 0)
    for s in range(1, cols):
        total = total + contract(whole(q_all, s), tests_of(s), 0, 0)
    gw_ref[...] = total * factor

    total = g_part[0].astype(F32)
    for s in range(1, cols):
        drain(g_recv.at[s - 1], gr_recv.at[s])
        total = total + g_recv[s - 1].astype(F32)
    gt_ref[...] = (total * factor).astype(BF16)

    for s in range(cols):
        for full, sc, ga in ((m_all, ms_send, ma_send), (q_all, qs_send, qa_send)):
            drain(full.at[s, pl.ds(0, rows - 1)], sc.at[s])
            drain(full.at[s, pl.ds(0, rows - 1)], ga.at[s])
        if s:
            drain(t_ref, t_send.at[s])
            drain(l_part.at[s - 1], l_send.at[s])
            drain(d_all.at[0], d_send.at[s])
            drain(g_part.at[s], g_send.at[s])


def local(rows, cols, programs, tests, weight, labels):
    (pr, eb), (tb, fb) = programs.shape, tests.shape
    sub = tb // rows
    vmem = pl.BlockSpec(memory_space=pltpu.VMEM)
    block = lambda *shape: pltpu.VMEM(shape, BF16)
    return pl.pallas_call(
        functools.partial(kernel, rows, cols),
        out_shape=(
            jax.ShapeDtypeStruct((pr, eb), BF16),
            jax.ShapeDtypeStruct((tb, fb), BF16),
            jax.ShapeDtypeStruct((eb, fb), F32),
        ),
        in_specs=[vmem] * 4,
        out_specs=(vmem,) * 3,
        scratch_shapes=[
            block(cols - 1, tb, fb),
            block(cols, rows, sub, eb), block(cols, rows - 1, sub, eb), block(cols, rows, sub, eb),
            block(cols - 1, pr, tb), block(cols - 1, pr, tb),
            block(cols, pr, tb),
            block(cols, rows, sub, eb), block(cols, rows - 1, sub, eb), block(cols, rows, sub, eb),
            block(cols, tb, fb), block(cols - 1, tb, fb),
            pltpu.VMEM((pr, tb), F32),
            pltpu.SemaphoreType.DMA((8, cols)),
            pltpu.SemaphoreType.DMA((8, cols)),
        ],
        compiler_params=pltpu.CompilerParams(
            collective_id=0, has_side_effects=True, vmem_limit_bytes=48 * 1024 * 1024
        ),
    )(programs, tests, weight, labels)


def solution(mesh):
    placed = (
        P(("grp", "row"), "col"),
        P(("grp", "col"), "row"),
        P("col", "row"),
        P(("grp", "row"), "col"),
    )
    return jax.shard_map(
        functools.partial(local, mesh.shape["row"], mesh.shape["col"]),
        mesh=mesh,
        in_specs=placed,
        out_specs=(P(("grp", "row"), "col"), P(("grp", "col"), "row"), P(("grp", "col"), "row")),
        check_vma=False,
    )
```

time: 237 us -> 102 us (0.43)
  waiting for transfers between devices: 203 us -> 0 us
  Pallas kernels: 0 us -> 94.4 us
  matrix products: 14.1 us -> 0 us
  between operations: 14.2 us -> 0.65 us
  local copies, waits for them, and re-layouts: 3.38 us -> 6.26 us
    pallas_call x0 -> x1, Pallas kernels: none -> 94.4 us  [local(): pl.pallas_call(functools.partial(kernel, rows, cols), out_shape=(jax.Shap...]
    reduce_scatter x3 -> x0, waiting for transfers between devices: 76.1 us -> none  [the longest x1 26 us: local(): lax.psum_scatter(weight_part.astype(jnp.bfloat16), 'row', scatter_dimensi...]
    all_gather x3 -> x0, waiting for transfers between devices: 74 us -> none  [the longest x1 28.8 us: local(): projected = lax.all_gather(share, 'col', axis=0, tiled=True)]
    psum x1 -> x0, waiting for transfers between devices: 51.3 us -> none  [local(): summed = lax.psum(partial_sums.astype(jnp.bfloat16), 'col')]
    dot_general x6 -> x0, matrix products: 14.1 us -> none  [the longest x4 9.43 us: contract(): lax.dot_general(left, right, (((left_dim,), (right_dim,)), ((), ())), pre...]
    unnamed x11, local copies, waits for them, and re-layouts: 3.38 us -> 6.26 us
  transfers between devices with their start and end apart: 7 -> 0, of which waited for: 7 -> 0; matrix products, arithmetic and copies ran while one was open for 3% -> 0% of each run, Pallas kernels for 0% -> 0%
where the time goes in v1:
time: 102 us; the launch traced here: 101 us
  Pallas kernels  94.4 us (93%)
  local copies, waits for them, and re-layouts  6.26 us (6%)
    pallas_call x1, Pallas kernels, local(): pl.pallas_call(functools.partial(kernel, rows, cols), out_shape=(jax.Shap...  94.4 us
    unnamed x11, local copies, waits for them, and re-layouts  6.26 us

profile of v1, /device:TPU:9, one launch (start us, length us, event | category | flops | bytes accessed | tf_op | source)
XLA Modules:
  0.0 101.3 jit_solution(7193750149080435124)
XLA Ops:
  0.6 0.0 copy-start
  0.6 1.0 %copy-done = bf16[512,512]{1,0:T(8,128)(2,1)S(1)} copy-done((bf16[512,512]{1,0:T(8,128)(2,1)S(1)}, bf16[512,512]{1,0:T(8,128)(2,1)}, u32[]{:S(2)}) %copy-start) | copy-done | bytes 524312
  1.7 0.0 copy-start.1
  1.7 0.9 copy-done.1
  2.6 0.0 copy-start.2
  2.6 0.9 copy-done.2
  3.6 0.0 copy-start.3
  3.6 0.9 copy-done.3
  4.5 94.4 %shard_map.67 = (bf16[256,512]{1,0:T(8,128)(2,1)S(1)}, bf16[256,512]{1,0:T(8,128)(2,1)S(1)}, f32[512,512]{1,0:T(8,128)S(1)}) custom-call(bf16[256,512]{1,0:T(8,128)(2,1)S(1)} %copy-done.1, bf16[256,512]{1,0:T(8,128)(2,1)S(1)} %copy-done.2, bf16[512,512]{1,0:T(8,128)(2,1)S(1)} %copy-done, s32[256,256]{1,0:T(8,128)S(1)} %copy-done.3), custom_call_target="tpu_custom_call" | custom-call | tf_op jit(solution)/shard_map/pallas_call | solution.py:202
  99.0 0.7 copy.10
  99.7 0.7 copy.11
  100.4 1.0 copy.12
Async XLA Ops:
  0.6 1.0 %copy-start = (bf16[512,512]{1,0:T(8,128)(2,1)S(1)}, bf16[512,512]{1,0:T(8,128)(2,1)}, u32[]{:S(2)}) copy-start(bf16[512,512]{1,0:T(8,128)(2,1)} %w_ref.1) | copy-start | bytes 1572868
  1.7 0.9 copy-start.1
  2.6 0.9 copy-start.2
  3.6 0.9 copy-start.3

commit v2 on v0

v2 whole, which is shorter than its diff:
```python
import functools
import math

import jax
import jax.numpy as jnp
from jax import lax
from jax.experimental import pallas as pl
from jax.experimental.pallas import tpu as pltpu
from jax.sharding import PartitionSpec as P

E = 2048
MESH = pl.DeviceIdType.MESH
BF16 = jnp.bfloat16
F32 = jnp.float32
M_ORDER = (0, 2, 1, 3)
D_SEND = (2, 1, 3)
Q_ORDER = (2, 1, 3, 0)


def contract(left, right, left_dim, right_dim):
    return lax.dot_general(
        left, right, (((left_dim,), (right_dim,)), ((), ())), preferred_element_type=F32
    )


def partner(index, step):
    bit = 1
    while bit <= step:
        if step & bit:
            index = index + bit - 2 * bit * (lax.div(index, bit) % 2)
        bit *= 2
    return index


def kernel(
    rows, cols,
    p_hbm, t_hbm, w_hbm, l_hbm,
    gp_ref, gt_ref, gw_ref,
    p_ref, w_ref, l_ref,
    t_all, m_part, m_sib, m_half, m_far, m_all, l_part, l_recv, d_all,
    q_part, q_sib, q_half, q_far, q_all, g_part, g_recv,
    acc, load, send, recv,
):
    factor = 1.0 / math.sqrt(E)
    r, c = lax.axis_index("row"), lax.axis_index("col")
    t_s, m1_s, m2_s, m3_s, l_s, d_s, q1_s, q2_s, q3_s, g_s = (send.at[i] for i in range(10))
    t_r, m1_r, m2_r, m3_r, l_r, d_r, q1_r, q2_r, q3_r, g_r = (recv.at[i] for i in range(10))
    core, chips = lax.rem(r, 2), rows // 2
    sibling = {"row": r + 1 - 2 * core}
    relay = cols == 4
    inner = lax.div(c + 1, 2) == 1

    loads = [
        pltpu.make_async_copy(a, b, load.at[i])
        for i, (a, b) in enumerate(((w_hbm, w_ref), (t_hbm, t_all.at[0]), (p_hbm, p_ref), (l_hbm, l_ref)))
    ]
    for one in loads:
        one.start()

    def far(k):
        return {"row": lax.rem(r + 2 * k, rows)}

    def col_peer(s):
        return {"col": partner(c, s)}

    barrier = pltpu.get_barrier_semaphore()
    for peer in [sibling] + [far(k) for k in range(1, chips)] + [col_peer(s) for s in range(1, cols)]:
        pl.semaphore_signal(barrier, inc=1, device_id=peer, device_id_type=MESH)
    pl.semaphore_wait(barrier, chips + cols - 1)

    def push(src, dst, ssem, rsem, peer):
        pltpu.make_async_remote_copy(
            src_ref=src, dst_ref=dst, send_sem=ssem, recv_sem=rsem, device_id=peer, device_id_type=MESH
        ).start()

    def drain(ref, sem):
        pltpu.make_async_copy(ref, ref, sem).wait()

    def send_tests(s):
        push(t_hbm, t_all.at[s], t_s.at[s], t_r.at[s], col_peer(s))

    if relay:
        send_tests(2)
        pl.when(inner)(lambda: send_tests(3))
        send_tests(1)
    else:
        for s in range(1, cols):
            send_tests(s)

    def share(value, part, s, ssem, rsem, sib):
        part[s] = value.astype(BF16).reshape(part.shape[1:])
        push(part.at[s, 1 - core], sib.at[s], ssem.at[s], rsem.at[s], sibling)

    def cross(part, sib, half, away, s, rsem1, ssem2, rsem2):
        drain(sib.at[s], rsem1.at[s])
        half[s] = (part[s, core].astype(F32) + sib[s].astype(F32)).astype(BF16)
        for k in range(1, chips):
            push(half.at[s], away.at[s, k - 1], ssem2.at[s], rsem2.at[s], far(k))

    def finish(half, away, full, s, rsem2, ssem3, rsem3):
        drain(away.at[s], rsem2.at[s])
        total = half[s].astype(F32)
        for k in range(chips - 1):
            total = total + away[s, k].astype(F32)
        full[s, core] = total.astype(BF16)
        push(full.at[s, core], full.at[s, core], ssem3.at[s], rsem3.at[s], sibling)

    def whole(full, s):
        return full[s].reshape(full.shape[1] * full.shape[2], full.shape[3])

    def m_make(s):
        if s:
            drain(t_all.at[s], t_r.at[s])
            if relay and s == 2:
                pl.when(inner)(lambda: push(t_all.at[2], t_all.at[3], t_s.at[0], t_r.at[3], col_peer(1)))
        share(contract(t_all[s], w_ref[...], 1, 1), m_part, s, m1_s, m1_r, m_sib)
        cross(m_part, m_sib, m_half, m_far, s, m1_r, m2_s, m2_r)

    def m_use(s):
        finish(m_half, m_far, m_all, s, m2_r, m3_s, m3_r)
        if s == 0:
            loads[2].wait()
        drain(m_half.at[s], m3_r.at[s])
        part = contract(p_ref[...], whole(m_all, s), 1, 1)
        if s == 0:
            acc[...] = part
        else:
            l_part[s - 1] = part.astype(BF16)
            push(l_part.at[s - 1], l_recv.at[s - 1], l_s.at[s], l_r.at[s], col_peer(s))

    loads[0].wait()
    loads[1].wait()
    order = M_ORDER if relay else list(range(cols))
    for i, s in enumerate(order):
        m_make(s)
        if i:
            m_use(order[i - 1])
    m_use(order[-1])

    loads[3].wait()
    logits = acc[...]
    for s in range(1, cols):
        drain(l_recv.at[s - 1], l_r.at[s])
        logits = logits + l_recv[s - 1].astype(F32)
    d_all[0] = (jax.nn.sigmoid(logits * factor) - l_ref[...].astype(F32)).astype(BF16)
    for s in (D_SEND if relay else range(1, cols)):
        push(d_all.at[0], d_all.at[s], d_s.at[s], d_r.at[s], col_peer(s))

    def q_make(s):
        if s:
            drain(d_all.at[s], d_r.at[s])
        share(contract(d_all[s], p_ref[...], 0, 0), q_part, s, q1_s, q1_r, q_sib)
        cross(q_part, q_sib, q_half, q_far, s, q1_r, q2_s, q2_r)

    def q_use(s):
        finish(q_half, q_far, q_all, s, q2_r, q3_s, q3_r)
        drain(q_half.at[s], q3_r.at[s])
        g_part[s] = contract(whole(q_all, s), w_ref[...], 1, 0).astype(BF16)
        if s:
            push(g_part.at[s], g_recv.at[s - 1], g_s.at[s], g_r.at[s], col_peer(s))

    order = Q_ORDER if relay else list(range(cols))
    for i, s in enumerate(order):
        q_make(s)
        if i:
            q_use(order[i - 1])
    q_use(order[-1])

    total = contract(d_all[0], whole(m_all, 0), 1, 0)
    for s in range(1, cols):
        total = total + contract(d_all[s], whole(m_all, s), 1, 0)
    gp_ref[...] = (total * factor).astype(BF16)
    total = contract(whole(q_all, 0), t_all[0], 0, 0)
    for s in range(1, cols):
        total = total + contract(whole(q_all, s), t_all[s], 0, 0)
    gw_ref[...] = total * factor

    total = g_part[0].astype(F32)
    for s in range(1, cols):
        drain(g_recv.at[s - 1], g_r.at[s])
        total = total + g_recv[s - 1].astype(F32)
    gt_ref[...] = (total * factor).astype(BF16)

    for s in range(cols):
        for away, half, s1, s2, s3 in ((m_far, m_half, m1_s, m2_s, m3_s), (q_far, q_half, q1_s, q2_s, q3_s)):
            drain(half.at[s], s1.at[s])
            drain(away.at[s], s2.at[s])
            drain(half.at[s], s3.at[s])
        if s:
            drain(l_part.at[s - 1], l_s.at[s])
            drain(d_all.at[0], d_s.at[s])
            drain(g_part.at[s], g_s.at[s])
            if not (relay and s == 3):
                drain(t_all.at[s], t_s.at[s])
    if relay:
        @pl.when(inner)
        def _():
            drain(t_all.at[3], t_s.at[3])
            drain(t_all.at[2], t_s.at[0])


def local(rows, cols, programs, tests, weight, labels):
    (pr, eb), (tb, fb) = programs.shape, tests.shape
    half, chips = tb // 2, rows // 2
    vmem, hbm = pl.BlockSpec(memory_space=pltpu.VMEM), pl.BlockSpec(memory_space=pl.ANY)
    block = lambda *shape: pltpu.VMEM(shape, BF16)
    reduce = [
        block(cols, 2, half, eb), block(cols, half, eb), block(cols, half, eb),
        block(cols, chips - 1, half, eb), block(cols, 2, half, eb),
    ]
    return pl.pallas_call(
        functools.partial(kernel, rows, cols),
        out_shape=(
            jax.ShapeDtypeStruct((pr, eb), BF16),
            jax.ShapeDtypeStruct((tb, fb), BF16),
            jax.ShapeDtypeStruct((eb, fb), F32),
        ),
        in_specs=[hbm] * 4,
        out_specs=(vmem,) * 3,
        scratch_shapes=[
            block(pr, eb), block(eb, fb), pltpu.VMEM((pr, tb), jnp.int32),
            block(cols, tb, fb),
            *reduce,
            block(cols - 1, pr, tb), block(cols - 1, pr, tb),
            block(cols, pr, tb),
            *reduce,
            block(cols, tb, fb), block(cols - 1, tb, fb),
            pltpu.VMEM((pr, tb), F32),
            pltpu.SemaphoreType.DMA((4,)),
            pltpu.SemaphoreType.DMA((10, cols)),
            pltpu.SemaphoreType.DMA((10, cols)),
        ],
        compiler_params=pltpu.CompilerParams(collective_id=0, has_side_effects=True),
    )(programs, tests, weight, labels)


def solution(mesh):
    placed = (
        P(("grp", "row"), "col"),
        P(("grp", "col"), "row"),
        P("col", "row"),
        P(("grp", "row"), "col"),
    )
    return jax.shard_map(
        functools.partial(local, mesh.shape["row"], mesh.shape["col"]),
        mesh=mesh,
        in_specs=placed,
        out_specs=(P(("grp", "row"), "col"), P(("grp", "col"), "row"), P(("grp", "col"), "row")),
        check_vma=False,
    )
```

time: 237 us -> 81.3 us (0.34)
  waiting for transfers between devices: 203 us -> 0 us
  Pallas kernels: 0 us -> 75 us
  matrix products: 14.1 us -> 0 us
  between operations: 14.2 us -> 0.65 us
    reduce_scatter x3 -> x0, waiting for transfers between devices: 76.1 us -> none  [the longest x1 26 us: local(): lax.psum_scatter(weight_part.astype(jnp.bfloat16), 'row', scatter_dimensi...]
    pallas_call x0 -> x1, Pallas kernels: none -> 75 us  [local(): pl.pallas_call(functools.partial(kernel, rows, cols), out_shape=(jax.Shap...]
    all_gather x3 -> x0, waiting for transfers between devices: 74 us -> none  [the longest x1 28.8 us: local(): projected = lax.all_gather(share, 'col', axis=0, tiled=True)]
    psum x1 -> x0, waiting for transfers between devices: 51.3 us -> none  [local(): summed = lax.psum(partial_sums.astype(jnp.bfloat16), 'col')]
    dot_general x6 -> x0, matrix products: 14.1 us -> none  [the longest x4 9.43 us: contract(): lax.dot_general(left, right, (((left_dim,), (right_dim,)), ((), ())), pre...]
  transfers between devices with their start and end apart: 7 -> 0, of which waited for: 7 -> 0; matrix products, arithmetic and copies ran while one was open for 3% -> 0% of each run, Pallas kernels for 0% -> 0%
where the time goes in v2:
time: 81.3 us; the launch traced here: 80 us
  Pallas kernels  75 us (92%)
  local copies, waits for them, and re-layouts  4.4 us (5%)
    pallas_call x1, Pallas kernels, local(): pl.pallas_call(functools.partial(kernel, rows, cols), out_shape=(jax.Shap...  75 us
    unnamed x5, local copies, waits for them, and re-layouts  4.4 us

profile of v2, /device:TPU:9, one launch (start us, length us, event | category | flops | bytes accessed | tf_op | source)
XLA Modules:
  0.0 80.0 jit_solution(13265852581971884031)
XLA Ops:
  0.6 75.0 %shard_map.67 = (bf16[256,512]{1,0:T(8,128)(2,1)}, bf16[256,512]{1,0:T(8,128)(2,1)}, f32[512,512]{1,0:T(8,128)}) custom-call(bf16[256,512]{1,0:T(8,128)(2,1)} %p_hbm.1, bf16[256,512]{1,0:T(8,128)(2,1)} %t_hbm.1, bf16[512,512]{1,0:T(8,128)(2,1)} %w_hbm.1, s32[256,256]{1,0:T(8,128)} %l_hbm.1), custom_call_target="tpu_custom_call" | custom-call | tf_op jit(solution)/shard_map/pallas_call | solution.py:211
  75.6 0.0 copy-start
  75.6 1.8 %copy.10 = bf16[256,512]{1,0:T(8,128)(2,1)} copy(bf16[256,512]{1,0:T(8,128)(2,1)} %get-tuple-element.6) | data formatting | bytes 524288
  77.4 1.7 %copy.11 = bf16[256,512]{1,0:T(8,128)(2,1)} copy(bf16[256,512]{1,0:T(8,128)(2,1)} %get-tuple-element.7) | data formatting | bytes 524288
  79.1 0.0 copy-done
  79.1 1.0 %copy.12 = f32[512,512]{1,0:T(8,128)} copy(f32[512,512]{1,0:T(8,128)S(1)} %copy-done) | data formatting | bytes 2097152
Async XLA Ops:
  75.6 3.4 %copy-start = (f32[512,512]{1,0:T(8,128)S(1)}, f32[512,512]{1,0:T(8,128)}, u32[]{:S(2)}) copy-start(f32[512,512]{1,0:T(8,128)} %get-tuple-element.8) | copy-start | bytes 3145732

commit v3 on v0

v3 whole, which is shorter than its diff:
```python
import functools
import math

import jax
import jax.numpy as jnp
from jax import lax
from jax.experimental import pallas as pl
from jax.experimental.pallas import tpu as pltpu
from jax.sharding import PartitionSpec as P

E = 2048
MESH = pl.DeviceIdType.MESH
BF16 = jnp.bfloat16
F32 = jnp.float32
M_ORDER = (0, 2, 1, 3)
Q_ORDER = (0, 2, 1, 3)
PARTS = 2
D_EARLY = 3
D_AFTER = 2


def contract(left, right, left_dim, right_dim):
    return lax.dot_general(
        left, right, (((left_dim,), (right_dim,)), ((), ())), preferred_element_type=F32
    )


def partner(index, step):
    bit = 1
    while bit <= step:
        if step & bit:
            index = index + bit - 2 * bit * (lax.div(index, bit) % 2)
        bit *= 2
    return index


def kernel(
    rows, cols,
    p_hbm, t_hbm, w_hbm, l_hbm,
    gp_ref, gt_ref, gw_ref,
    p_ref, w_ref, l_ref,
    t_all, m_part, m_sib, m_half, m_far, m_all, l_part, l_recv, d_all,
    q_part, q_sib, q_half, q_far, q_all, g_part, g_recv,
    acc, load, send, recv,
):
    factor = 1.0 / math.sqrt(E)
    r, c = lax.axis_index("row"), lax.axis_index("col")
    t_s, m1_s, m2_s, m3_s, l_s, d_s, q1_s, q2_s, q3_s, g_s = (send.at[i] for i in range(10))
    t_r, m1_r, m2_r, m3_r, l_r, d_r, q1_r, q2_r, q3_r, g_r = (recv.at[i] for i in range(10))
    core, chips = lax.rem(r, 2), rows // 2
    sibling = {"row": r + 1 - 2 * core}
    relay = cols == 4
    middle = lax.rem(lax.div(c + 1, 2), 2)
    inner, outer = middle == 1, middle == 0

    loads = [
        pltpu.make_async_copy(a, b, load.at[i])
        for i, (a, b) in enumerate(((w_hbm, w_ref), (t_hbm.at[pl.ds(0, t_all.shape[1])], t_all.at[0]), (p_hbm, p_ref), (l_hbm, l_ref)))
    ]
    loads += [
        pltpu.make_async_copy(t_hbm.at[pl.ds(h * t_all.shape[1], t_all.shape[1])], t_all.at[h], load.at[3 + h])
        for h in range(1, PARTS)
    ]
    for one in loads:
        one.start()

    def far(k):
        return {"row": lax.rem(r + 2 * k, rows)}

    def col_peer(s):
        return {"col": partner(c, s)}

    barrier = pltpu.get_barrier_semaphore()
    for peer in [sibling] + [far(k) for k in range(1, chips)] + [col_peer(s) for s in range(1, cols)]:
        pl.semaphore_signal(barrier, inc=1, device_id=peer, device_id_type=MESH)
    pl.semaphore_wait(barrier, chips + cols - 1)

    def push(src, dst, ssem, rsem, peer):
        pltpu.make_async_remote_copy(
            src_ref=src, dst_ref=dst, send_sem=ssem, recv_sem=rsem, device_id=peer, device_id_type=MESH
        ).start()

    def drain(ref, sem):
        pltpu.make_async_copy(ref, ref, sem).wait()

    def at(s, h):
        return s * PARTS + h

    def forward(full, s, h, sems, semr):
        if relay and s == 2:
            @pl.when(inner)
            def _():
                push(full.at[at(2, h)], full.at[at(3, h)], sems.at[at(0, h)], semr.at[at(3, h)], col_peer(1))

    def spread(src, full, h, sems, semr):
        def one(s):
            push(src, full.at[at(s, h)], sems.at[at(s, h)], semr.at[at(s, h)], col_peer(s))

        if relay:
            one(2)
            pl.when(inner)(lambda: one(3))
            one(1)
        else:
            for s in range(1, cols):
                one(s)

    step = t_all.shape[1]
    for h in range(PARTS):
        spread(t_hbm.at[pl.ds(h * step, step)], t_all, h, t_s, t_r)

    def cross(value, part, sib, half, away, b, s1, r1, s2, r2):
        part[b] = value.astype(BF16).reshape(part.shape[1:])
        push(part.at[b, 1 - core], sib.at[b], s1.at[b], r1.at[b], sibling)
        drain(sib.at[b], r1.at[b])
        half[b] = (part[b, core].astype(F32) + sib[b].astype(F32)).astype(BF16)
        for k in range(1, chips):
            push(half.at[b], away.at[b, k - 1], s2.at[b], r2.at[b], far(k))

    def finish(half, away, full, b, r2, s3, r3):
        drain(away.at[b], r2.at[b])
        total = half[b].astype(F32)
        for k in range(chips - 1):
            total = total + away[b, k].astype(F32)
        full[b, core] = total.astype(BF16)
        push(full.at[b, core], full.at[b, core], s3.at[b], r3.at[b], sibling)
        drain(half.at[b], r3.at[b])

    def give(value, part, came, s, h, sems, semr):
        b = at(s, h)
        part[b] = value.astype(BF16)
        peer = col_peer(s)
        if relay and s == 2:
            peer = {"col": middle * partner(c, 2) + (1 - middle) * partner(c, 1)}
        if relay and s == 3:
            @pl.when(inner)
            def _():
                drain(came.at[at(2, h)], semr.at[at(2, h)])
                part[b] = (value + came[at(2, h)].astype(F32)).astype(BF16)
        push(part.at[b], came.at[b], sems.at[b], semr.at[b], peer)

    def collect(total, came, h, semr):
        for s in range(1, cols):
            b = at(s, h)
            if relay and s == 2:
                @pl.when(outer)
                def _():
                    drain(came.at[b], semr.at[b])
                total = total + jnp.where(outer, came[b].astype(F32), 0.0)
            else:
                drain(came.at[b], semr.at[b])
                total = total + came[b].astype(F32)
        return total

    def whole(full, b):
        return full[b].reshape(full.shape[1] * full.shape[2], full.shape[3])

    def m_make(s, h):
        b = at(s, h)
        if s:
            drain(t_all.at[b], t_r.at[b])
            forward(t_all, s, h, t_s, t_r)
        cross(contract(t_all[b], w_ref[...], 1, 1), m_part, m_sib, m_half, m_far, b, m1_s, m1_r, m2_s, m2_r)

    def m_use(s, h):
        b = at(s, h)
        finish(m_half, m_far, m_all, b, m2_r, m3_s, m3_r)
        part = contract(p_ref[...], whole(m_all, b), 1, 1)
        if s:
            give(part, l_part, l_recv, s, h, l_s, l_r)
        else:
            acc[h] = part

    def d_make(h):
        logits = collect(acc[h], l_recv, h, l_r)
        labels = l_ref[:, h * step:(h + 1) * step].astype(F32)
        d_all[at(0, h)] = (jax.nn.sigmoid(logits * factor) - labels).astype(BF16)
        spread(d_all.at[at(0, h)], d_all, h, d_s, d_r)

    def q_make(s, h):
        b = at(s, h)
        if s:
            drain(d_all.at[b], d_r.at[b])
            forward(d_all, s, h, d_s, d_r)
        cross(contract(d_all[b], p_ref[...], 0, 0), q_part, q_sib, q_half, q_far, b, q1_s, q1_r, q2_s, q2_r)

    def q_use(s, h):
        b = at(s, h)
        finish(q_half, q_far, q_all, b, q2_r, q3_s, q3_r)
        part = contract(whole(q_all, b), w_ref[...], 1, 0)
        if s:
            give(part, g_part, g_recv, s, h, g_s, g_r)
        else:
            g_part[b] = part.astype(BF16)

    for one in loads:
        one.wait()
    makes = {"m": m_make, "q": q_make}
    uses = {"m": m_use, "q": q_use}
    order = M_ORDER if relay else tuple(range(cols))
    late = Q_ORDER if relay else tuple(range(cols))
    work = [("m", s, h) for h in range(PARTS) for s in order]
    work += [("q", s, h) for h in range(PARTS) for s in late]
    waiting, left = [], {h: cols for h in range(PARTS)}
    made = set()

    def use_first():
        kind, s, h = waiting.pop(0)
        uses[kind](s, h)
        if kind == "m":
            left[h] -= 1

    def settle(h):
        if h not in made and left[h] == 0:
            made.add(h)
            d_make(h)

    for i, (kind, s, h) in enumerate(work):
        if kind == "q" and s == late[D_AFTER if h == 0 else 0]:
            for g in range(h + 2 if h + 1 < PARTS else h + 1):
                while left[g]:
                    use_first()
                settle(g)
        elif kind == "q" and h not in made:
            while left[h]:
                use_first()
            settle(h)
        if kind == "m" and h and s == order[D_EARLY]:
            while left[h - 1]:
                use_first()
            settle(h - 1)
        makes[kind](s, h)
        waiting.append((kind, s, h))
        if len(waiting) > 1:
            use_first()
    while waiting:
        use_first()

    blocks = [at(s, h) for s in range(cols) for h in range(PARTS)]
    total = contract(d_all[0], whole(m_all, 0), 1, 0)
    for b in blocks[1:]:
        total = total + contract(d_all[b], whole(m_all, b), 1, 0)
    gp_ref[...] = (total * factor).astype(BF16)
    total = contract(whole(q_all, 0), t_all[0], 0, 0)
    for b in blocks[1:]:
        total = total + contract(whole(q_all, b), t_all[b], 0, 0)
    gw_ref[...] = total * factor
    for h in range(PARTS):
        total = collect(g_part[at(0, h)].astype(F32), g_recv, h, g_r)
        gt_ref[pl.ds(h * step, step)] = (total * factor).astype(BF16)

    for s in range(cols):
        for h in range(PARTS):
            b = at(s, h)
            for away, half, s1, s2, s3 in ((m_far, m_half, m1_s, m2_s, m3_s), (q_far, q_half, q1_s, q2_s, q3_s)):
                drain(half.at[b], s1.at[b])
                drain(away.at[b], s2.at[b])
                drain(half.at[b], s3.at[b])
            if s:
                drain(l_part.at[b], l_s.at[b])
                drain(g_part.at[b], g_s.at[b])
                if not (relay and s == 3):
                    drain(d_all.at[b], d_s.at[b])
                    drain(t_all.at[b], t_s.at[b])
    if relay:
        @pl.when(inner)
        def _():
            for h in range(PARTS):
                for full, sem in ((t_all, t_s), (d_all, d_s)):
                    drain(full.at[at(3, h)], sem.at[at(3, h)])
                    drain(full.at[at(2, h)], sem.at[at(0, h)])


def passed(a, b, c, x, y, z):
    x[...], y[...], z[...] = a[...], b[...], c[...]


def local(rows, cols, programs, tests, weight, labels):
    (pr, eb), (tb, fb) = programs.shape, tests.shape
    blocks, step, chips = cols * PARTS, tb // PARTS, rows // 2
    half = step // 2
    vmem, hbm = pl.BlockSpec(memory_space=pltpu.VMEM), pl.BlockSpec(memory_space=pl.ANY)
    block = lambda *shape: pltpu.VMEM((blocks, *shape), BF16)
    reduce = [block(2, half, eb), block(half, eb), block(half, eb), block(chips - 1, half, eb), block(2, half, eb)]
    outs = pl.pallas_call(
        functools.partial(kernel, rows, cols),
        out_shape=(
            jax.ShapeDtypeStruct((pr, eb), BF16),
            jax.ShapeDtypeStruct((tb, fb), BF16),
            jax.ShapeDtypeStruct((eb, fb), F32),
        ),
        in_specs=[hbm] * 4,
        out_specs=(vmem,) * 3,
        scratch_shapes=[
            pltpu.VMEM((pr, eb), BF16), pltpu.VMEM((eb, fb), BF16), pltpu.VMEM((pr, tb), jnp.int32),
            block(step, fb),
            *reduce,
            block(pr, step), block(pr, step),
            block(pr, step),
            *reduce,
            block(step, fb), block(step, fb),
            pltpu.VMEM((PARTS, pr, step), F32),
            pltpu.SemaphoreType.DMA((3 + PARTS,)),
            pltpu.SemaphoreType.DMA((10, blocks)),
            pltpu.SemaphoreType.DMA((10, blocks)),
        ],
        compiler_params=pltpu.CompilerParams(collective_id=0, has_side_effects=True),
    )(programs, tests, weight, labels)
    return pl.pallas_call(
        passed,
        out_shape=tuple(jax.ShapeDtypeStruct(x.shape, x.dtype) for x in outs),
        in_specs=[vmem] * 3,
        out_specs=(vmem,) * 3,
    )(*outs)


def solution(mesh):
    placed = (
        P(("grp", "row"), "col"),
        P(("grp", "col"), "row"),
        P("col", "row"),
        P(("grp", "row"), "col"),
    )
    return jax.shard_map(
        functools.partial(local, mesh.shape["row"], mesh.shape["col"]),
        mesh=mesh,
        in_specs=placed,
        out_specs=(P(("grp", "row"), "col"), P(("grp", "col"), "row"), P(("grp", "col"), "row")),
        check_vma=False,
    )
```

time: 237 us -> 74.4 us (0.31)
  waiting for transfers between devices: 203 us -> 0 us
  Pallas kernels: 0 us -> 72.7 us
  matrix products: 14.1 us -> 0 us
  between operations: 14.2 us -> 0.64 us
  local copies, waits for them, and re-layouts: 3.38 us -> 0 us
    reduce_scatter x3 -> x0, waiting for transfers between devices: 76.1 us -> none  [the longest x1 26 us: local(): lax.psum_scatter(weight_part.astype(jnp.bfloat16), 'row', scatter_dimensi...]
    all_gather x3 -> x0, waiting for transfers between devices: 74 us -> none  [the longest x1 28.8 us: local(): projected = lax.all_gather(share, 'col', axis=0, tiled=True)]
    pallas_call x0 -> x2, Pallas kernels: none -> 72.7 us  [the longest x1 70.2 us: local(): pl.pallas_call(functools.partial(kernel, rows, cols), out_shape=(jax.Shap...]
    psum x1 -> x0, waiting for transfers between devices: 51.3 us -> none  [local(): summed = lax.psum(partial_sums.astype(jnp.bfloat16), 'col')]
    dot_general x6 -> x0, matrix products: 14.1 us -> none  [the longest x4 9.43 us: contract(): lax.dot_general(left, right, (((left_dim,), (right_dim,)), ((), ())), pre...]
    unnamed x11 -> x0, local copies, waits for them, and re-layouts: 3.38 us -> none
  transfers between devices with their start and end apart: 7 -> 0, of which waited for: 7 -> 0; matrix products, arithmetic and copies ran while one was open for 3% -> 0% of each run, Pallas kernels for 0% -> 0%
where the time goes in v3:
time: 74.4 us; the launch traced here: 73.4 us
  Pallas kernels  72.7 us (98%)
    pallas_call x1, Pallas kernels, local(): pl.pallas_call(functools.partial(kernel, rows, cols), out_shape=(jax.Shap...  70.2 us
    pallas_call x1, Pallas kernels, local(): pl.pallas_call(passed, out_shape=tuple((jax.ShapeDtypeStruct(x.shape, x.d...  2.55 us

profile of v3, /device:TPU:9, one launch (start us, length us, event | category | flops | bytes accessed | tf_op | source)
XLA Modules:
  0.0 73.4 jit_solution(5155203520223638214)
XLA Ops:
  0.6 70.2 %shard_map.67 = (bf16[256,512]{1,0:T(8,128)(2,1)}, bf16[256,512]{1,0:T(8,128)(2,1)}, f32[512,512]{1,0:T(8,128)}) custom-call(bf16[256,512]{1,0:T(8,128)(2,1)} %p_hbm.1, bf16[256,512]{1,0:T(8,128)(2,1)} %t_hbm.1, bf16[512,512]{1,0:T(8,128)(2,1)} %w_hbm.1, s32[256,256]{1,0:T(8,128)} %l_hbm.1), custom_call_target="tpu_custom_call" | custom-call | tf_op jit(solution)/shard_map/pallas_call | solution.py:284
  70.8 2.6 %shard_map.68 = (bf16[256,512]{1,0:T(8,128)(2,1)}, bf16[256,512]{1,0:T(8,128)(2,1)}, f32[512,512]{1,0:T(8,128)}) custom-call(bf16[256,512]{1,0:T(8,128)(2,1)} %get-tuple-element.6.a, bf16[256,512]{1,0:T(8,128)(2,1)} %get-tuple-element.7.b, f32[512,512]{1,0:T(8,128)} %get-tuple-element.8.c), custom_call_target="tpu_custom_call" | custom-call | tf_op jit(solution)/shard_map/pallas_call | solution.py:308
